TPU v7x, 256 devices: a whole 4x4x8 slice. The times are simulated.
256 devices in a mesh: dp: 4 (over y), seq: 16 (over z, core), fsdp: 4 (over x).
Axes of the slice: x: 4, y: 4, z: 8, core: 2. Of those that a mesh axis runs over, the one named last changes fastest.
Arguments:
- signal: bfloat16 [16, 2048, 1024], P(('dp', 'fsdp'), 'seq'), may hold values from -100 to 100
- w_query: bfloat16 [1024, 512], P('fsdp'), may hold values from -1 to 1
- w_key: bfloat16 [1024, 512], P('fsdp'), may hold values from -1 to 1
- w_value: bfloat16 [1024, 512], P('fsdp'), may hold values from -0.1875 to 0.1875
- w_output: bfloat16 [1024, 512], P('fsdp'), may hold values from -0.25 to 0.25
- upstream: bfloat16 [16, 2048, 1024], P(('dp', 'fsdp'), 'seq'), may hold values from -6 to 6
Outputs:
- output: bfloat16 [16, 2048, 1024], P(('dp', 'fsdp'), 'seq')
- grad_signal: bfloat16 [16, 2048, 1024], P(('dp', 'fsdp'), 'seq')
- grad_query: float32 [1024, 512], P('fsdp')
- grad_key: float32 [1024, 512], P('fsdp')
- grad_value: float32 [1024, 512], P('fsdp')
- grad_output: float32 [1024, 512], P('fsdp')
All inputs are finite; a program needn't handle non-finite values.
Results may differ from a plain program's by a relative error of at most 0.02.
The roundings to bfloat16 on the way count: a program that leaves them out, or rounds other values in their place, can miss the bound.
Values may be sent and summed in bfloat16 or wider, within the bound.
No kernel may reach another device: no remote copies, remote signals or barrier semaphores. Data moves between devices by JAX's collectives and lax.ppermute only.
A program may use at most 128 MiB of HBM per device.

v0:
```python
import jax
import jax.numpy as jnp
from jax import lax
from jax.sharding import PartitionSpec as P

HEADS = 8
HSIZE = 64


def normalize(frame_rows):
    widened = frame_rows.astype(jnp.float32)
    centre = widened - jnp.mean(widened, axis=-1, keepdims=True)
    variance = jnp.mean(centre * centre, axis=-1, keepdims=True)
    inverse = lax.rsqrt(variance + 1e-05)
    return (centre * inverse, inverse)


def split_heads(matrix):
    return matrix.reshape(matrix.shape[0], HEADS, HSIZE)


def dot_across(left, right):
    return lax.dot_general(
        left, right, (((0,), (0,)), ((), ())), preferred_element_type=jnp.float32
    )


def dot_against(left, right):
    return lax.dot_general(
        left, right, (((1,), (1,)), ((), ())), preferred_element_type=jnp.float32
    )


def body(signal, w_query, w_key, w_value, w_output, upstream):
    q_weight, k_weight, v_weight, o_weight = (
        lax.all_gather(w_query, "fsdp", axis=0, tiled=True),
        lax.all_gather(w_key, "fsdp", axis=0, tiled=True),
        lax.all_gather(w_value, "fsdp", axis=0, tiled=True),
        lax.all_gather(w_output, "fsdp", axis=0, tiled=True),
    )
    score_scale = HSIZE ** (-0.5)
    frame_rows = signal[0]
    grad_frames = upstream[0]
    local_frames = frame_rows.shape[0]
    width_heads = q_weight.shape[1]
    normed_f, inverse = normalize(frame_rows)
    normed = normed_f.astype(jnp.bfloat16)
    queries = jnp.dot(normed, q_weight, preferred_element_type=jnp.float32).astype(jnp.bfloat16)
    key_rows = jnp.dot(normed, k_weight, preferred_element_type=jnp.float32).astype(jnp.bfloat16)
    value_rows = jnp.dot(normed, v_weight, preferred_element_type=jnp.float32).astype(jnp.bfloat16)
    all_keys, all_values = (
        lax.all_gather(key_rows, "seq", axis=0, tiled=True),
        lax.all_gather(value_rows, "seq", axis=0, tiled=True),
    )
    query_heads = split_heads(queries)
    key_heads = split_heads(all_keys)
    value_heads = split_heads(all_values)
    scores = (
        jnp.einsum("qhs,khs->hqk", query_heads, key_heads, preferred_element_type=jnp.float32)
        * score_scale
    )
    row_max = jnp.max(scores, axis=-1, keepdims=True)
    exponent = jnp.exp(scores - row_max)
    row_total = jnp.sum(exponent, axis=-1, keepdims=True)
    attention = exponent / row_total
    attn_weights = attention.astype(jnp.bfloat16)
    context = jnp.einsum(
        "hqk,khs->qhs", attn_weights, value_heads, preferred_element_type=jnp.float32
    )
    context = context.reshape(local_frames, width_heads).astype(jnp.bfloat16)
    projected = dot_against(context, o_weight)
    output_rows = (frame_rows.astype(jnp.float32) + projected).astype(jnp.bfloat16)
    grad_context = jnp.dot(grad_frames, o_weight, preferred_element_type=jnp.float32).astype(
        jnp.bfloat16
    )
    grad_heads = split_heads(grad_context)
    grad_attention = jnp.einsum(
        "qhs,khs->hqk", grad_heads, value_heads, preferred_element_type=jnp.float32
    )
    row_delta = jnp.sum(attention * grad_attention, axis=-1, keepdims=True)
    grad_scores = (attention * (grad_attention - row_delta) * score_scale).astype(jnp.bfloat16)
    grad_queries = jnp.einsum(
        "hqk,khs->qhs", grad_scores, key_heads, preferred_element_type=jnp.float32
    )
    grad_queries = grad_queries.reshape(local_frames, width_heads).astype(jnp.bfloat16)
    term_keys = jnp.einsum(
        "hqk,qhs->khs", grad_scores, query_heads, preferred_element_type=jnp.float32
    )
    term_values = jnp.einsum(
        "hqk,qhs->khs", attn_weights, grad_heads, preferred_element_type=jnp.float32
    )
    summed = lax.psum_scatter(
        jnp.concatenate(
            [
                term_keys.reshape(local_frames * lax.axis_size("seq"), width_heads),
                term_values.reshape(local_frames * lax.axis_size("seq"), width_heads),
            ],
            axis=1,
        ).astype(jnp.bfloat16),
        "seq",
        scatter_dimension=0,
        tiled=True,
    ).astype(jnp.float32)
    grad_keys = summed[:, :width_heads].astype(jnp.bfloat16)
    grad_values = summed[:, width_heads:].astype(jnp.bfloat16)
    grad_normed = (
        dot_against(grad_queries, q_weight)
        + dot_against(grad_keys, k_weight)
        + dot_against(grad_values, v_weight)
    )
    grad_mean = jnp.mean(grad_normed, axis=-1, keepdims=True)
    grad_along = jnp.mean(grad_normed * normed_f, axis=-1, keepdims=True)
    grad_rows = grad_frames.astype(jnp.float32) + inverse * (
        grad_normed - grad_mean - normed_f * grad_along
    )
    grad_rows = grad_rows.astype(jnp.bfloat16)
    shares = lax.psum_scatter(
        jnp.concatenate(
            [
                dot_across(normed, grad_queries),
                dot_across(normed, grad_keys),
                dot_across(normed, grad_values),
                dot_across(grad_frames, context),
            ],
            axis=1,
        ).astype(jnp.bfloat16),
        "fsdp",
        scatter_dimension=0,
        tiled=True,
    ).astype(jnp.float32)
    totals = lax.psum(shares, ("dp", "seq"))
    token_count = (
        signal.shape[0]
        * lax.axis_size("dp")
        * lax.axis_size("fsdp")
        * local_frames
        * lax.axis_size("seq")
    )
    totals = totals * token_count ** (-0.5)
    return (
        output_rows[None],
        grad_rows[None],
        totals[:, :width_heads],
        totals[:, width_heads : 2 * width_heads],
        totals[:, 2 * width_heads : 3 * width_heads],
        totals[:, 3 * width_heads :],
    )


def solution(mesh):
    placed = (
        P(("dp", "fsdp"), "seq", None),
        P("fsdp", None),
        P("fsdp", None),
        P("fsdp", None),
        P("fsdp", None),
        P(("dp", "fsdp"), "seq", None),
    )
    return jax.shard_map(
        body,
        mesh=mesh,
        in_specs=placed,
        out_specs=(
            P(("dp", "fsdp"), "seq", None),
            P(("dp", "fsdp"), "seq", None),
            P("fsdp", None),
            P("fsdp", None),
            P("fsdp", None),
            P("fsdp", None),
        ),
        check_vma=False,
    )
```

profile of v0, /device:TPU:2, one launch (start us, length us, event | category | flops | bytes accessed | tf_op | source)
XLA Modules:
  0.0 645.6 jit_solution(7578981338521241008)
XLA Ops:
  7.2 0.7 all-gather.13.cloned.1.call-update
  7.9 0.7 all-gather.7.cloned.1.call-update
  8.7 0.7 all-gather.11.cloned.1.call-update
  9.4 0.5 all-gather.17.cloned.1.call-update
  10.0 1.1 convert_reduce_fusion
  11.1 1.2 fusion.43
  12.3 26.0 %all-gather.13.cloned.1.call-done = bf16[1024,512]{1,0:T(8,128)(2,1)} async-done(((bf16[256,512]{1,0:T(8,128)(2,1)}), bf16[1024,512]{1,0:T(8,128)(2,1)}) %all-gather.13.cloned.1.call-update) | async-done | bytes 1048592 | tf_op jit(solution)/shard_map/all_gather | solution.py:37
  38.2 2.3 convolution_convert_fusion.6
  40.6 26.5 %all-gather.7.cloned.1.call-done = bf16[1024,512]{1,0:T(8,128)(2,1)} async-done(((bf16[256,512]{1,0:T(8,128)(2,1)}), bf16[1024,512]{1,0:T(8,128)(2,1)}) %all-gather.7.cloned.1.call-update) | async-done | bytes 1048592 | tf_op jit(solution)/shard_map/all_gather | solution.py:38
  67.1 2.3 convolution_convert_fusion.8
  69.5 26.5 %all-gather.11.cloned.1.call-done = bf16[1024,512]{1,0:T(8,128)(2,1)} async-done(((bf16[256,512]{1,0:T(8,128)(2,1)}), bf16[1024,512]{1,0:T(8,128)(2,1)}) %all-gather.11.cloned.1.call-update) | async-done | bytes 1048592 | tf_op jit(solution)/shard_map/all_gather | solution.py:36
  96.0 1.7 convolution_convert_fusion.7
  97.8 26.9 %all-gather.17.cloned.1.call-done = bf16[1024,512]{1,0:T(8,128)(2,1)} async-done(((bf16[256,512]{1,0:T(8,128)(2,1)}), bf16[1024,512]{1,0:T(8,128)(2,1)}) %all-gather.17.cloned.1.call-update) | async-done | bytes 1048592 | tf_op jit(solution)/shard_map/all_gather | solution.py:39
  124.7 1.6 convolution_convert_fusion.5
  126.4 41.5 %all-gather.15.cloned.1.call-done = bf16[2048,512]{1,0:T(8,128)(2,1)} async-done(((bf16[128,512]{1,0:T(8,128)(2,1)}), bf16[2048,512]{1,0:T(8,128)(2,1)}) %all-gather.15.cloned.1.call-update) | async-done | bytes 2097168 | tf_op jit(solution)/shard_map/all_gather | solution.py:52
  167.9 2.9 copy.34
  170.9 4.7 fusion.69
  175.6 32.5 %all-gather.9.cloned.1.call-done = bf16[2048,512]{1,0:T(8,128)(2,1)} async-done(((bf16[128,512]{1,0:T(8,128)(2,1)}), bf16[2048,512]{1,0:T(8,128)(2,1)}) %all-gather.9.cloned.1.call-update) | async-done | bytes 2097168 | tf_op jit(solution)/shard_map/all_gather | solution.py:53
  208.0 2.9 copy.32
  211.0 5.4 fusion.70
  216.4 0.7 copy-done.7
  217.0 2.2 convolution_convert_fusion
  219.3 16.7 %fusion.15 = bf16[8,64,2048]{2,1,0:T(8,128)(2,1)} fusion(bf16[128,8,64]{0,2,1:T(8,128)(2,1)S(1)} %bitcast.102, f32[8,128,2048]{2,1,0:T(8,128)} %fusion.70, f32[8,128,2048]{2,1,0:T(8,128)} %get-tuple-element.31, f32[8,128]{1,0:T(8,128)S(1)} %get-tuple-element.30), kind=kOutput, calls=%fused_computation.14 | convolution fusion | flops 284167168 | bytes 19009536 | tf_op jit(solution)/shard_map/hqk,qhs->khs/dot_general | solution.py:86
  236.0 4.8 pad_maximum_fusion
  240.8 6.4 copy.40
  247.2 0.2 reduce-scatter.5.cloned.1.call-start
  247.4 5.0 fusion.24
  252.5 0.6 copy-done.6
  253.1 1.4 fusion.21
  254.5 17.2 %fusion.27 = bf16[8,64,128]{2,1,0:T(8,128)(2,1)S(1)} fusion(bf16[2048,8,64]{0,2,1:T(8,128)(2,1)} %bitcast.92, f32[8,128,2048]{2,1,0:T(8,128)} %fusion.70, f32[8,128,2048]{2,1,0:T(8,128)} %get-tuple-element.31, f32[8,128]{1,0:T(8,128)S(1)} %get-tuple-element.30), kind=kOutput, calls=%fused_computation.30 | convolution fusion | flops 283184128 | bytes 19009536 | tf_op jit(solution)/shard_map/hqk,khs->qhs/dot_general | solution.py:82
  271.7 1.5 convolution_convert_fusion.3
  273.3 35.8 %reduce-scatter.7.cloned.1.call-done = bf16[128,1024]{1,0:T(8,128)(2,1)} async-done(((bf16[2048,1024]{1,0:T(8,128)(2,1)}), bf16[128,1024]{1,0:T(8,128)(2,1)}) %reduce-scatter.7.cloned.1.call-update) | async-done | bytes 262160
  309.0 1.4 convolution_convert_fusion.1
  310.5 1.5 convolution_convert_fusion.2
  312.0 3.6 pad_maximum_fusion.1
  315.6 2.5 fusion.23
  318.1 0.5 fusion.71
  318.6 1.4 convolution_add_fusion.1
  320.0 1.5 fusion.67
  321.5 1.9 fusion.48
  323.4 39.0 %reduce-scatter.5.cloned.1.call-done = bf16[256,2048]{0,1:T(8,128)(2,1)} async-done(((bf16[1024,2048]{0,1:T(8,128)(2,1)}), bf16[256,2048]{0,1:T(8,128)(2,1)}) %reduce-scatter.5.cloned.1.call-update) | async-done | bytes 1048592 | tf_op jit(solution)/shard_map/reduce_scatter | solution.py:117
  362.4 272.1 %all-reduce.1 = f32[256,2048]{0,1:T(8,128)S(1)} all-reduce(bf16[256,2048]{0,1:T(8,128)(2,1)} %reduce-scatter.5.cloned.1.call-done), channel_id=1, replica_groups=mesh['dp'=4,'seq'=16,'fsdp'=4] {'dp','seq'}, use_global_device_ids=true, to_apply=%region_9.0 | all-reduce | flops 524288 | bytes 3145728 | tf_op jit(solution)/shard_map/psum | solution.py:131
  634.4 0.2 broadcast_multiply_fusion
  634.6 0.1 fusion.68
  634.8 1.0 copy.36
  635.8 1.0 copy.37
  636.8 1.0 copy.38
  637.8 1.0 copy.39
  (30 shorter events, 0.6 us)
Async XLA Ops:
  7.2 31.1 %all-gather.13.cloned.1.call-start = ((), (), s32[]{:S(2)}) async-start(), calls=%async_computation.5 | async-start | bytes 1310720 | tf_op jit(solution)/shard_map/all_gather | solution.py:37
  7.9 59.2 %all-gather.7.cloned.1.call-start = ((), (), s32[]{:S(2)}) async-start(), calls=%async_computation.2 | async-start | bytes 1310720 | tf_op jit(solution)/shard_map/all_gather | solution.py:38
  8.6 87.3 %all-gather.11.cloned.1.call-start = ((), (), s32[]{:S(2)}) async-start(), calls=%async_computation.4 | async-start | bytes 1310720 | tf_op jit(solution)/shard_map/all_gather | solution.py:36
  9.4 115.3 %all-gather.17.cloned.1.call-start = ((), (), s32[]{:S(2)}) async-start(), calls=%async_computation.7 | async-start | bytes 1310720 | tf_op jit(solution)/shard_map/all_gather | solution.py:39
  10.0 158.0 %all-gather.15.cloned.1.call-start = ((), (), s32[]{:S(2)}) async-start(), calls=%async_computation.6 | async-start | bytes 2228224 | tf_op jit(solution)/shard_map/all_gather | solution.py:52
  40.6 167.5 %all-gather.9.cloned.1.call-start = ((), (), s32[]{:S(2)}) async-start(), calls=%async_computation.3 | async-start | bytes 2228224 | tf_op jit(solution)/shard_map/all_gather | solution.py:53
  69.5 239.6 %reduce-scatter.7.cloned.1.call-start = ((), (), s32[]{:S(2)}) async-start(), calls=%async_computation.9 | async-start | bytes 4456448
  170.9 4.7 copy-start.5
  211.0 6.1 copy-start.7
  247.2 5.9 copy-start.4
  247.2 115.2 %reduce-scatter.5.cloned.1.call-start = ((), (), s32[]{:S(2)}) async-start(), calls=%async_computation.8 | async-start | bytes 5242880 | tf_op jit(solution)/shard_map/reduce_scatter | solution.py:117
  252.5 0.7 copy-start.6
  254.5 17.2 %copy-start = (bf16[1,128,1024]{2,1,0:T(8,128)(2,1)S(1)}, bf16[1,128,1024]{2,1,0:T(8,128)(2,1)}, u32[]{:S(2)}) copy-start(bf16[1,128,1024]{2,1,0:T(8,128)(2,1)} %param.6) | copy-start | bytes 786436
  273.2 44.8 %copy-start.3 = (bf16[1024,512]{1,0:T(8,128)(2,1)S(1)}, bf16[1024,512]{1,0:T(8,128)(2,1)}, u32[]{:S(2)}) copy-start(bf16[1024,512]{1,0:T(8,128)(2,1)} %all-gather.11.cloned.1.call-done) | copy-start | bytes 3145732
  310.5 8.1 %copy-start.1 = (bf16[1024,512]{1,0:T(8,128)(2,1)S(1)}, bf16[1024,512]{1,0:T(8,128)(2,1)}, u32[]{:S(2)}) copy-start(bf16[1024,512]{1,0:T(8,128)(2,1)} %all-gather.13.cloned.1.call-done) | copy-start | bytes 3145732
  312.0 8.0 %copy-start.2 = (bf16[1024,512]{1,0:T(8,128)(2,1)S(1)}, bf16[1024,512]{1,0:T(8,128)(2,1)}, u32[]{:S(2)}) copy-start(bf16[1024,512]{1,0:T(8,128)(2,1)} %all-gather.7.cloned.1.call-done) | copy-start | bytes 3145732
Sparse Core Ops, SparseCore 0:
  9.8 28.4 all-gather.12
  40.1 27.0 all-gather.6
  68.9 27.0 all-gather.10
  97.6 27.0 all-gather.16
  126.9 40.9 all-gather.14
  170.2 37.8 all-gather.8
  247.3 61.6 reduce-scatter.6
  315.7 46.6 reduce-scatter.4
where the time goes:
time: 646 us
  blocking collectives  272 us (42%)
  waiting for transfers between devices  257 us (40%)
  matrix products  70.9 us (11%)
  local copies, waits for them, and re-layouts  17.9 us (3%)
  between operations  14.3 us (2%)
  other arithmetic  12.7 us (2%)
    psum x1, blocking collectives, body(): totals = lax.psum(shares, ('dp', 'seq'))  272 us
    all_gather x1, waiting for transfers between devices, body(): lax.all_gather(key_rows, 'seq', axis=0, tiled=True)  41.5 us
    reduce_scatter x1, waiting for transfers between devices, body(): lax.psum_scatter(jnp.concatenate([dot_across(normed, grad_queries), dot_a...  39 us
    unnamed x9, waiting for transfers between devices  38.4 us
    all_gather x1, waiting for transfers between devices, body(): lax.all_gather(value_rows, 'seq', axis=0, tiled=True)  32.5 us
    all_gather x1, waiting for transfers between devices, body(): lax.all_gather(w_output, 'fsdp', axis=0, tiled=True)  26.9 us
    all_gather x1, waiting for transfers between devices, body(): lax.all_gather(w_query, 'fsdp', axis=0, tiled=True)  26.5 us
    all_gather x1, waiting for transfers between devices, body(): lax.all_gather(w_value, 'fsdp', axis=0, tiled=True)  26.5 us
  transfers between devices with their start and end apart: 8, of which 8 were waited for; matrix products, arithmetic and copies ran while one was open for 8% of the time, Pallas kernels for 0%

commit v1 on v0

--- a/solution.py
+++ b/solution.py
@@ -128,7 +128,7 @@
         scatter_dimension=0,
         tiled=True,
     ).astype(jnp.float32)
-    totals = lax.psum(shares, ("dp", "seq"))
+    totals = lax.psum(lax.psum(shares, "dp"), "seq")
     token_count = (
         signal.shape[0]
         * lax.axis_size("dp")

time: 646 us -> 534 us (0.83)
  blocking collectives: 272 us -> 43.8 us
  waiting for transfers between devices: 257 us -> 374 us
    psum x1, blocking collectives: 272 us -> 43.8 us  [body(): totals = lax.psum(lax.psum(shares, 'dp'), 'seq')]
    psum x0 -> x1, waiting for transfers between devices: none -> 111 us  [body(): totals = lax.psum(lax.psum(shares, 'dp'), 'seq')]
    unnamed x9 -> x10, waiting for transfers between devices: 38.4 us -> 40.4 us
  transfers between devices with their start and end apart: 8 -> 9, of which waited for: 8 -> 9; matrix products, arithmetic and copies ran while one was open for 8% -> 9% of each run, Pallas kernels for 0% -> 0%
where the time goes in v1:
time: 534 us; the launch traced here: 533 us
  waiting for transfers between devices  374 us (70%)
  matrix products  69.9 us (13%)
  blocking collectives  43.8 us (8%)
  local copies, waits for them, and re-layouts  17.9 us (3%)
  between operations  14.1 us (3%)
  other arithmetic  12.1 us (2%)
    psum x1, waiting for transfers between devices, body(): totals = lax.psum(lax.psum(shares, 'dp'), 'seq')  111 us
    psum x1, blocking collectives, body(): totals = lax.psum(lax.psum(shares, 'dp'), 'seq')  43.8 us
    reduce_scatter x1, waiting for transfers between devices, body(): lax.psum_scatter(jnp.concatenate([dot_across(normed, grad_queries), dot_a...  42.9 us
    all_gather x1, waiting for transfers between devices, body(): lax.all_gather(key_rows, 'seq', axis=0, tiled=True)  41.5 us
    unnamed x10, waiting for transfers between devices  40.4 us
    all_gather x1, waiting for transfers between devices, body(): lax.all_gather(value_rows, 'seq', axis=0, tiled=True)  32.5 us
    all_gather x1, waiting for transfers between devices, body(): lax.all_gather(w_output, 'fsdp', axis=0, tiled=True)  26.9 us
    all_gather x1, waiting for transfers between devices, body(): lax.all_gather(w_query, 'fsdp', axis=0, tiled=True)  26.5 us
  transfers between devices with their start and end apart: 9, of which 9 were waited for; matrix products, arithmetic and copies ran while one was open for 9% of the time, Pallas kernels for 0%

profile of v1, /device:TPU:2, one launch (start us, length us, event | category | flops | bytes accessed | tf_op | source)
XLA Modules:
  0.0 532.7 jit_solution(1724166600069690899)
XLA Ops:
  7.2 0.7 all-gather.13.cloned.1.call-update
  7.9 0.7 all-gather.7.cloned.1.call-update
  8.7 0.7 all-gather.11.cloned.1.call-update
  9.4 0.5 all-gather.17.cloned.1.call-update
  10.0 1.1 convert_reduce_fusion
  11.1 1.2 fusion.43
  12.3 26.0 %all-gather.13.cloned.1.call-done = bf16[1024,512]{1,0:T(8,128)(2,1)} async-done(((bf16[256,512]{1,0:T(8,128)(2,1)}), bf16[1024,512]{1,0:T(8,128)(2,1)}) %all-gather.13.cloned.1.call-update) | async-done | bytes 1048592 | tf_op jit(solution)/shard_map/all_gather | solution.py:37
  38.2 2.3 convolution_convert_fusion.6
  40.6 26.5 %all-gather.7.cloned.1.call-done = bf16[1024,512]{1,0:T(8,128)(2,1)} async-done(((bf16[256,512]{1,0:T(8,128)(2,1)}), bf16[1024,512]{1,0:T(8,128)(2,1)}) %all-gather.7.cloned.1.call-update) | async-done | bytes 1048592 | tf_op jit(solution)/shard_map/all_gather | solution.py:38
  67.1 2.3 convolution_convert_fusion.8
  69.5 26.5 %all-gather.11.cloned.1.call-done = bf16[1024,512]{1,0:T(8,128)(2,1)} async-done(((bf16[256,512]{1,0:T(8,128)(2,1)}), bf16[1024,512]{1,0:T(8,128)(2,1)}) %all-gather.11.cloned.1.call-update) | async-done | bytes 1048592 | tf_op jit(solution)/shard_map/all_gather | solution.py:36
  96.0 1.7 convolution_convert_fusion.7
  97.8 26.9 %all-gather.17.cloned.1.call-done = bf16[1024,512]{1,0:T(8,128)(2,1)} async-done(((bf16[256,512]{1,0:T(8,128)(2,1)}), bf16[1024,512]{1,0:T(8,128)(2,1)}) %all-gather.17.cloned.1.call-update) | async-done | bytes 1048592 | tf_op jit(solution)/shard_map/all_gather | solution.py:39
  124.7 1.6 convolution_convert_fusion.5
  126.4 41.5 %all-gather.15.cloned.1.call-done = bf16[2048,512]{1,0:T(8,128)(2,1)} async-done(((bf16[128,512]{1,0:T(8,128)(2,1)}), bf16[2048,512]{1,0:T(8,128)(2,1)}) %all-gather.15.cloned.1.call-update) | async-done | bytes 2097168 | tf_op jit(solution)/shard_map/all_gather | solution.py:52
  167.9 2.9 copy.34
  170.9 4.7 fusion.69
  175.6 32.5 %all-gather.9.cloned.1.call-done = bf16[2048,512]{1,0:T(8,128)(2,1)} async-done(((bf16[128,512]{1,0:T(8,128)(2,1)}), bf16[2048,512]{1,0:T(8,128)(2,1)}) %all-gather.9.cloned.1.call-update) | async-done | bytes 2097168 | tf_op jit(solution)/shard_map/all_gather | solution.py:53
  208.1 2.9 copy.32
  211.0 5.4 %fusion.70 = f32[8,128,2048]{2,1,0:T(8,128)} fusion(bf16[128,8,64]{0,2,1:T(8,128)(2,1)S(1)} %bitcast.99, bf16[2048,8,64]{0,2,1:T(8,128)(2,1)S(1)} %bitcast.89), kind=kOutput, calls=%fused_computation.76 | convolution fusion | flops 268435456 | bytes 10616832 | tf_op jit(solution)/shard_map/qhs,khs->hqk/dot_general | solution.py:77
  216.4 0.7 copy-done.8
  217.0 2.2 convolution_convert_fusion
  219.2 16.8 %fusion.15 = bf16[8,64,2048]{2,1,0:T(8,128)(2,1)} fusion(bf16[128,8,64]{0,2,1:T(8,128)(2,1)S(1)} %bitcast.102, f32[8,128,2048]{2,1,0:T(8,128)} %fusion.70, f32[8,128,2048]{2,1,0:T(8,128)} %get-tuple-element.31, f32[8,128]{1,0:T(8,128)S(1)} %get-tuple-element.30), kind=kOutput, calls=%fused_computation.14 | convolution fusion | flops 284167168 | bytes 19009536 | tf_op jit(solution)/shard_map/hqk,qhs->khs/dot_general | solution.py:86
  236.0 4.8 pad_maximum_fusion
  240.8 6.4 %copy.40 = bf16[2048,1024]{1,0:T(8,128)(2,1)} copy(bf16[2048,1024]{0,1:T(8,128)(2,1)} %pad_maximum_fusion) | data formatting | bytes 8388608
  247.2 0.2 reduce-scatter.5.cloned.1.call-start
  247.5 5.0 fusion.24
  252.5 0.6 copy-done.7
  253.2 0.4 fusion.21
  253.6 17.2 %fusion.27 = bf16[8,64,128]{2,1,0:T(8,128)(2,1)S(1)} fusion(bf16[2048,8,64]{0,2,1:T(8,128)(2,1)} %bitcast.92, f32[8,128,2048]{2,1,0:T(8,128)} %fusion.70, f32[8,128,2048]{2,1,0:T(8,128)} %get-tuple-element.31, f32[8,128]{1,0:T(8,128)S(1)} %get-tuple-element.30), kind=kOutput, calls=%fused_computation.30 | convolution fusion | flops 283184128 | bytes 19009536 | tf_op jit(solution)/shard_map/hqk,khs->qhs/dot_general | solution.py:82
  270.8 0.5 convolution_convert_fusion.3
  271.3 37.7 %reduce-scatter.7.cloned.1.call-done = bf16[128,1024]{1,0:T(8,128)(2,1)} async-done(((bf16[2048,1024]{1,0:T(8,128)(2,1)}), bf16[128,1024]{1,0:T(8,128)(2,1)}) %reduce-scatter.7.cloned.1.call-update) | async-done | bytes 262160
  309.1 1.4 convolution_convert_fusion.1
  310.5 1.4 convolution_convert_fusion.2
  311.9 2.3 pad_maximum_fusion.1
  314.3 2.6 fusion.23
  317.0 1.3 fusion.71
  318.2 42.9 %reduce-scatter.5.cloned.1.call-done = bf16[256,2048]{0,1:T(8,128)(2,1)} async-done(((bf16[1024,2048]{0,1:T(8,128)(2,1)}), bf16[256,2048]{0,1:T(8,128)(2,1)}) %reduce-scatter.5.cloned.1.call-update) | async-done | bytes 1048592 | tf_op jit(solution)/shard_map/reduce_scatter | solution.py:117
  361.1 43.8 %all-reduce.4 = f32[256,2048]{0,1:T(8,128)} all-reduce(bf16[256,2048]{0,1:T(8,128)(2,1)} %reduce-scatter.5.cloned.1.call-done), channel_id=1, replica_groups=mesh['dp'=4,'seq'=16,'fsdp'=4] {'dp'}, use_global_device_ids=true, to_apply=%region_9.0 | all-reduce | flops 524288 | bytes 3145728 | tf_op jit(solution)/shard_map/psum | solution.py:131
  405.0 1.6 convolution_add_fusion.1
  406.6 1.5 fusion.67
  408.1 1.0 fusion.48
  409.1 111.2 %all-reduce.3.cloned.1.call-done = f32[256,2048]{0,1:T(8,128)} async-done(((f32[256,2048]{0,1:T(8,128)}), f32[256,2048]{0,1:T(8,128)}) %all-reduce.3.cloned.1.call-update) | async-done | bytes 2097168 | tf_op jit(solution)/shard_map/psum | solution.py:131
  520.3 1.8 broadcast_multiply_fusion
  522.2 1.0 copy.36
  523.2 1.0 copy.37
  524.2 1.0 copy.38
  525.2 1.0 copy.39
  (35 shorter events, 0.8 us)
Async XLA Ops:
  7.2 31.1 %all-gather.13.cloned.1.call-start = ((), (), s32[]{:S(2)}) async-start(), calls=%async_computation.5 | async-start | bytes 1310720 | tf_op jit(solution)/shard_map/all_gather | solution.py:37
  7.9 59.2 %all-gather.7.cloned.1.call-start = ((), (), s32[]{:S(2)}) async-start(), calls=%async_computation.2 | async-start | bytes 1310720 | tf_op jit(solution)/shard_map/all_gather | solution.py:38
  8.6 87.3 %all-gather.11.cloned.1.call-start = ((), (), s32[]{:S(2)}) async-start(), calls=%async_computation.4 | async-start | bytes 1310720 | tf_op jit(solution)/shard_map/all_gather | solution.py:36
  9.4 115.3 %all-gather.17.cloned.1.call-start = ((), (), s32[]{:S(2)}) async-start(), calls=%async_computation.7 | async-start | bytes 1310720 | tf_op jit(solution)/shard_map/all_gather | solution.py:39
  10.0 158.0 %all-gather.15.cloned.1.call-start = ((), (), s32[]{:S(2)}) async-start(), calls=%async_computation.6 | async-start | bytes 2228224 | tf_op jit(solution)/shard_map/all_gather | solution.py:52
  40.6 167.5 %all-gather.9.cloned.1.call-start = ((), (), s32[]{:S(2)}) async-start(), calls=%async_computation.3 | async-start | bytes 2228224 | tf_op jit(solution)/shard_map/all_gather | solution.py:53
  69.5 239.6 %reduce-scatter.7.cloned.1.call-start = ((), (), s32[]{:S(2)}) async-start(), calls=%async_computation.10 | async-start | bytes 4456448
  170.9 4.7 copy-start.6
  211.0 6.1 %copy-start.8 = (f32[8,128,2048]{2,1,0:T(8,128)S(1)}, f32[8,128,2048]{2,1,0:T(8,128)}, u32[]{:S(2)}) copy-start(f32[8,128,2048]{2,1,0:T(8,128)} %get-tuple-element.31) | copy-start | bytes 25165828
  247.2 5.9 %copy-start.4 = (bf16[1,128,1024]{2,1,0:T(8,128)(2,1)S(1)}, bf16[1,128,1024]{2,1,0:T(8,128)(2,1)}, u32[]{:S(2)}) copy-start(bf16[1,128,1024]{2,1,0:T(8,128)(2,1)} %param.11) | copy-start | bytes 786436
  247.2 113.9 %reduce-scatter.5.cloned.1.call-start = ((), (), s32[]{:S(2)}) async-start(), calls=%async_computation.8 | async-start | bytes 5242880 | tf_op jit(solution)/shard_map/reduce_scatter | solution.py:117
  252.5 0.7 copy-start.7
  253.6 17.2 %copy-start = (bf16[1,128,1024]{2,1,0:T(8,128)(2,1)S(1)}, bf16[1,128,1024]{2,1,0:T(8,128)(2,1)}, u32[]{:S(2)}) copy-start(bf16[1,128,1024]{2,1,0:T(8,128)(2,1)} %param.6) | copy-start | bytes 786436
  271.3 45.6 %copy-start.3 = (bf16[1024,512]{1,0:T(8,128)(2,1)S(1)}, bf16[1024,512]{1,0:T(8,128)(2,1)}, u32[]{:S(2)}) copy-start(bf16[1024,512]{1,0:T(8,128)(2,1)} %all-gather.11.cloned.1.call-done) | copy-start | bytes 3145732
  314.3 90.7 %copy-start.1 = (bf16[1024,512]{1,0:T(8,128)(2,1)S(1)}, bf16[1024,512]{1,0:T(8,128)(2,1)}, u32[]{:S(2)}) copy-start(bf16[1024,512]{1,0:T(8,128)(2,1)} %all-gather.13.cloned.1.call-done) | copy-start | bytes 3145732
  314.3 92.3 %copy-start.2 = (bf16[1024,512]{1,0:T(8,128)(2,1)S(1)}, bf16[1024,512]{1,0:T(8,128)(2,1)}, u32[]{:S(2)}) copy-start(bf16[1024,512]{1,0:T(8,128)(2,1)} %all-gather.7.cloned.1.call-done) | copy-start | bytes 3145732
  314.3 206.0 %all-reduce.3.cloned.1.call-start = ((), (), s32[]{:S(2)}) async-start(), calls=%async_computation.9 | async-start | bytes 4194304 | tf_op jit(solution)/shard_map/psum | solution.py:131
  318.2 89.9 %copy-start.5 = (bf16[1,128,1024]{2,1,0:T(8,128)(2,1)S(1)}, bf16[1,128,1024]{2,1,0:T(8,128)(2,1)}, u32[]{:S(2)}) copy-start(bf16[1,128,1024]{2,1,0:T(8,128)(2,1)} %param.11) | copy-start | bytes 786436
Sparse Core Ops, SparseCore 0:
  9.8 28.4 all-gather.12
  40.1 27.0 all-gather.6
  68.9 27.0 all-gather.10
  97.6 27.0 all-gather.16
  126.9 40.9 all-gather.14
  170.2 37.8 all-gather.8
  247.3 61.6 reduce-scatter.6
  314.4 46.6 reduce-scatter.4
  405.1 115.1 all-reduce.2
